TPU v7x, 256 devices: a whole 4x4x8 slice. The times are simulated.
256 devices in a mesh: section: 8 (over z), neuron: 32 (over y, x, core).
Axes of the slice: x: 4, y: 4, z: 8, core: 2. Of those that a mesh axis runs over, the one named last changes fastest.
Arguments:
- inputs: bfloat16 [2, 256, 65536], P(None, None, 'neuron'), may hold values from -6 to 6
- weights: bfloat16 [16, 512, 3, 128, 128], P('section', 'neuron'), may hold values from -0.4375 to 0.4375
- bias: bfloat16 [16, 65536], P('section', 'neuron'), may hold values from -0.19921875 to 0.19921875
- offsets: int32 [16, 3], P('section'), may hold values from -3 to 3, as said below
Outputs:
- outputs: bfloat16 [2, 256, 65536], P(None, 'section', 'neuron')
Inputs may be any that keep to these rules, and one draw needn't show every extreme that they name: `offsets`: band 0 has offset 0; band 1 lies in 1 .. 3 and band 2 in -3 .. -1; some layer has 3 in band 1 and some layer -3 in band 2.
All inputs are finite; a program needn't handle non-finite values.
Results may differ from a plain program's by a relative error of at most 0.029.
Values may be sent and summed in bfloat16 or wider, within the bound.
A program may use at most 128 MiB of HBM per device.

v0:
```python
import jax
import jax.numpy as jnp
from jax import lax
from jax.sharding import PartitionSpec as P

HALO = 3


ceiling = 2.0


def padded(block, sides, width):
    for axis, dim in sides:
        count = lax.axis_size(axis)
        forward = [(i, i + 1) for i in range(count - 1)]
        forward.append((count - 1, 0))
        backward = [(target, source) for source, target in forward]
        low = lax.ppermute(
            lax.slice_in_dim(block, block.shape[dim] - width, None, axis=dim), axis, forward
        )
        high = lax.ppermute(lax.slice_in_dim(block, 0, width, axis=dim), axis, backward)
        block = jnp.concatenate([low, block, high], axis=dim)
    return block


def from_behind(value, axis, steps):
    count = lax.axis_size(axis)
    first, last = (max(0, -steps), min(count, count - steps))
    return lax.ppermute(value, axis, [(source, source + steps) for source in range(first, last)])


def spread(value, axis, source):
    kept = jnp.where(lax.axis_index(axis) == source, value, 0).astype(value.dtype)
    return lax.psum(kept, axis)


def shards(inputs, weights, bias, offsets):
    sections = lax.axis_size("section")
    section_index = lax.axis_index("section")
    micro_count, row_count, local_width = inputs.shape
    layer_count, block_count, band_count, block_size = (
        weights.shape[0],
        weights.shape[1],
        weights.shape[2],
        weights.shape[3],
    )
    packed = jnp.concatenate(
        [
            weights.reshape(layer_count, block_count, band_count * block_size, block_size),
            bias.reshape(layer_count, block_count, 1, block_size),
        ],
        axis=2,
    )
    table_edge = (packed.shape[1] - block_count) // 2

    def apply_layer(extended, table, layer_offsets, layer, margin):
        rows_here = extended.shape[0]
        out_blocks = block_count + 2 * margin
        first = table_edge - margin
        layer_weights = table[layer, first : first + out_blocks]
        summed = jnp.zeros((rows_here, out_blocks, block_size), jnp.float32)
        for band_index in range(band_count):
            start_col = (HALO + layer_offsets[layer, band_index]) * block_size
            shifted = lax.dynamic_slice_in_dim(
                extended, start_col, out_blocks * block_size, 1
            ).reshape(rows_here, out_blocks, block_size)
            block_weights = layer_weights[
                :, band_index * block_size : (band_index + 1) * block_size
            ]
            summed = summed + jnp.einsum(
                "rjk,jkn->rjn", shifted, block_weights, preferred_element_type=jnp.float32
            )
        bias_rows = layer_weights[:, band_count * block_size].astype(jnp.float32)
        preact = summed + bias_rows[None]
        return (
            jnp.clip(preact, 0.0, ceiling)
            .astype(jnp.bfloat16)
            .reshape(rows_here, out_blocks * block_size)
        )

    def run_section(current, table, layer_offsets):
        for layer in range(layer_count):
            extended = padded(current, (("neuron", 1),), HALO * block_size)
            current = apply_layer(extended, table, layer_offsets, layer, 0)
        return current

    share_rows = row_count // sections

    def advance(step_index, carry):
        incoming, finished_rows = carry
        arriving = lax.dynamic_index_in_dim(
            inputs, jnp.minimum(step_index, micro_count - 1), 0, keepdims=False
        )
        current = jnp.where(section_index == 0, arriving, incoming)
        produced = run_section(current, packed, offsets)
        slot_index = jnp.clip(step_index - (sections - 1), 0, micro_count - 1)
        finished = jnp.logical_and(section_index == sections - 1, step_index >= sections - 1)
        previous = lax.dynamic_index_in_dim(finished_rows, slot_index, 0, keepdims=False)
        finished_rows = lax.dynamic_update_index_in_dim(
            finished_rows, jnp.where(finished, produced, previous), slot_index, 0
        )
        incoming = from_behind(produced, "section", 1)
        return (incoming, finished_rows)

    initial = (
        jnp.zeros((row_count, local_width), jnp.bfloat16),
        jnp.zeros((micro_count, row_count, local_width), jnp.bfloat16),
    )
    incoming, finished_rows = lax.fori_loop(0, micro_count + sections - 1, advance, initial)
    everything = spread(finished_rows, "section", sections - 1)
    return lax.dynamic_slice_in_dim(everything, section_index * share_rows, share_rows, 1)


def solution(mesh):
    in_specs = (
        P(None, None, "neuron"),
        P("section", "neuron", None, None, None),
        P("section", "neuron"),
        P("section", None),
    )
    out_specs = P(None, "section", "neuron")
    return jax.shard_map(shards, mesh=mesh, in_specs=in_specs, out_specs=out_specs, check_vma=False)
```

profile of v0, /device:TPU:224, one launch (start us, length us, event | category | flops | bytes accessed | tf_op | source)
XLA Modules:
  0.0 549.0 jit_solution(16289615240674995746)
XLA Ops:
  12.7 2.2 pad_maximum_fusion.2
  14.9 5.1 copy.18
  20.0 1.6 broadcast_in_dim.19.clone2
  22.6 434.3 %while.17 = (s32[]{:T(128)}, bf16[256,2048]{0,1:T(8,128)(2,1)}, bf16[2,256,2048]{2,1,0:T(8,128)(2,1)}, pred[]{:T(512)}, bf16[2,256,2048]{2,1,0:T(8,128)(2,1)}, /...) while((s32[]{:T(128)}, bf16[256,2048]{0,1:T(8,128)(2,1)}, ...), condition=%wide.region_1.2_spmd, body=%wide.region_0.1_spmd.sunk | while | flops 820252672 | bytes 80798200 | solution.py:109
  22.6 1.7 constant_dynamic-slice_fusion.12
  26.2 4.7 collective-permute-start
  30.9 2.5 slice_bitcast_fusion.3
  34.1 5.2 collective-permute-done.1
  41.7 2.7 collective-permute-done.2
  44.4 5.3 collective-permute-done.3
  56.1 18.2 %collective-permute-done.4 = bf16[256,2048]{0,1:T(8,128)(2,1)} collective-permute-done((bf16[256,2048]{0,1:T(8,128)(2,1)}, bf16[256,2048]{0,1:T(8,128)(2,1)}, u32[]{:S(2)}, u32[]{:S(2)}) %collective-permute-start.4) | collective-permute-done | bytes 1048608 | tf_op jit(solution)/shard_map/while/body/eval_jaxpr/ppermute | solution.py:29
  74.3 1.7 constant_dynamic-slice_fusion.12
  78.5 2.5 slice_bitcast_fusion.3
  81.4 5.2 collective-permute-done.1
  89.0 2.7 collective-permute-done.2
  91.7 5.3 collective-permute-done.3
  103.4 18.2 %collective-permute-done.4 = bf16[256,2048]{0,1:T(8,128)(2,1)} collective-permute-done((bf16[256,2048]{0,1:T(8,128)(2,1)}, bf16[256,2048]{0,1:T(8,128)(2,1)}, u32[]{:S(2)}, u32[]{:S(2)}) %collective-permute-start.4) | collective-permute-done | bytes 1048608 | tf_op jit(solution)/shard_map/while/body/eval_jaxpr/ppermute | solution.py:29
  121.6 1.7 constant_dynamic-slice_fusion.12
  125.8 2.5 slice_bitcast_fusion.3
  128.6 5.1 collective-permute-done.1
  136.1 2.7 collective-permute-done.2
  138.8 5.3 collective-permute-done.3
  150.5 18.2 %collective-permute-done.4 = bf16[256,2048]{0,1:T(8,128)(2,1)} collective-permute-done((bf16[256,2048]{0,1:T(8,128)(2,1)}, bf16[256,2048]{0,1:T(8,128)(2,1)}, u32[]{:S(2)}, u32[]{:S(2)}) %collective-permute-start.4) | collective-permute-done | bytes 1048608 | tf_op jit(solution)/shard_map/while/body/eval_jaxpr/ppermute | solution.py:29
  168.8 1.7 constant_dynamic-slice_fusion.12
  173.0 2.5 slice_bitcast_fusion.3
  175.8 5.1 collective-permute-done.1
  183.3 2.7 collective-permute-done.2
  186.0 5.3 collective-permute-done.3
  192.5 1.6 clamp_convert_fusion.5
  197.7 18.2 %collective-permute-done.4 = bf16[256,2048]{0,1:T(8,128)(2,1)} collective-permute-done((bf16[256,2048]{0,1:T(8,128)(2,1)}, bf16[256,2048]{0,1:T(8,128)(2,1)}, u32[]{:S(2)}, u32[]{:S(2)}) %collective-permute-start.4) | collective-permute-done | bytes 1048608 | tf_op jit(solution)/shard_map/while/body/eval_jaxpr/ppermute | solution.py:29
  215.9 1.7 constant_dynamic-slice_fusion.12
  220.1 2.5 slice_bitcast_fusion.3
  223.0 5.1 collective-permute-done.1
  230.5 2.7 collective-permute-done.2
  233.2 5.3 collective-permute-done.3
  239.6 1.6 clamp_convert_fusion.5
  244.9 18.5 %collective-permute-done.4 = bf16[256,2048]{0,1:T(8,128)(2,1)} collective-permute-done((bf16[256,2048]{0,1:T(8,128)(2,1)}, bf16[256,2048]{0,1:T(8,128)(2,1)}, u32[]{:S(2)}, u32[]{:S(2)}) %collective-permute-start.4) | collective-permute-done | bytes 1048608 | tf_op jit(solution)/shard_map/while/body/eval_jaxpr/ppermute | solution.py:29
  263.4 1.7 constant_dynamic-slice_fusion.12
  267.5 2.5 slice_bitcast_fusion.3
  270.4 5.1 collective-permute-done.1
  277.9 2.7 collective-permute-done.2
  280.6 5.3 collective-permute-done.3
  292.3 19.4 %collective-permute-done.4 = bf16[256,2048]{0,1:T(8,128)(2,1)} collective-permute-done((bf16[256,2048]{0,1:T(8,128)(2,1)}, bf16[256,2048]{0,1:T(8,128)(2,1)}, u32[]{:S(2)}, u32[]{:S(2)}) %collective-permute-start.4) | collective-permute-done | bytes 1048608 | tf_op jit(solution)/shard_map/while/body/eval_jaxpr/ppermute | solution.py:29
  311.7 1.7 constant_dynamic-slice_fusion.12
  315.9 2.5 slice_bitcast_fusion.3
  318.8 5.1 collective-permute-done.1
  326.3 2.7 collective-permute-done.2
  329.0 5.3 collective-permute-done.3
  340.7 19.5 %collective-permute-done.4 = bf16[256,2048]{0,1:T(8,128)(2,1)} collective-permute-done((bf16[256,2048]{0,1:T(8,128)(2,1)}, bf16[256,2048]{0,1:T(8,128)(2,1)}, u32[]{:S(2)}, u32[]{:S(2)}) %collective-permute-start.4) | collective-permute-done | bytes 1048608 | tf_op jit(solution)/shard_map/while/body/eval_jaxpr/ppermute | solution.py:29
  360.1 1.7 constant_dynamic-slice_fusion.12
  364.3 2.5 slice_bitcast_fusion.3
  367.2 5.1 collective-permute-done.1
  374.7 2.7 collective-permute-done.2
  377.3 5.3 collective-permute-done.3
  390.3 18.2 %collective-permute-done.4 = bf16[256,2048]{0,1:T(8,128)(2,1)} collective-permute-done((bf16[256,2048]{0,1:T(8,128)(2,1)}, bf16[256,2048]{0,1:T(8,128)(2,1)}, u32[]{:S(2)}, u32[]{:S(2)}) %collective-permute-start.4) | collective-permute-done | bytes 1048608 | tf_op jit(solution)/shard_map/while/body/eval_jaxpr/ppermute | solution.py:29
  408.5 1.7 constant_dynamic-slice_fusion.12
  412.7 2.5 slice_bitcast_fusion.3
  415.5 5.1 collective-permute-done.1
  423.0 2.7 collective-permute-done.2
  425.7 5.3 collective-permute-done.3
  438.7 18.2 %collective-permute-done.4 = bf16[256,2048]{0,1:T(8,128)(2,1)} collective-permute-done((bf16[256,2048]{0,1:T(8,128)(2,1)}, bf16[256,2048]{0,1:T(8,128)(2,1)}, u32[]{:S(2)}, u32[]{:S(2)}) %collective-permute-start.4) | collective-permute-done | bytes 1048608 | tf_op jit(solution)/shard_map/while/body/eval_jaxpr/ppermute | solution.py:29
  456.9 3.1 broadcast_select_fusion
  460.0 80.5 %all-reduce.2.cloned.1.call-done = bf16[2,256,2048]{2,1,0:T(8,128)(2,1)} async-done(((bf16[2,256,2048]{2,1,0:T(8,128)(2,1)}), bf16[2,256,2048]{2,1,0:T(8,128)(2,1)}) %all-reduce.2.cloned.1.call-update) | async-done | bytes 2097168 | tf_op jit(solution)/shard_map/psum | solution.py:34
  540.4 1.7 constant_dynamic-slice_fusion.8
  (227 shorter events, 105.8 us)
Async XLA Ops:
  6.5 533.9 %all-reduce.2.cloned.1.call-start = ((), (), s32[]{:S(2)}) async-start(), calls=%async_computation | async-start | bytes 4194304 | tf_op jit(solution)/shard_map/psum | solution.py:34
  26.2 7.9 %collective-permute-start = (bf16[256,384]{0,1:T(8,128)(2,1)S(1)}, bf16[256,384]{0,1:T(8,128)(2,1)S(1)}, u32[]{:S(2)}, u32[]{:S(2)}) collective-permute-start(bf16[256,384]{0,1:T(8,128)(2,1)S(1)} %get-tuple-element.410), channel_id=1, source_target_pairs={{1,0},{2,1},{3,2},{4,3},{5,4},{6,5},{7,6},{8,7},{9,8},{10,9},{11,1... | collective-permute-start | bytes 589832 | tf_op jit(solution)/shard_map/while/body/eval_jaxpr/ppermute | solution.py:21
  30.9 8.4 %collective-permute-start.1 = (bf16[256,384]{0,1:T(8,128)(2,1)S(1)}, bf16[256,384]{0,1:T(8,128)(2,1)S(1)}, u32[]{:S(2)}, u32[]{:S(2)}) collective-permute-start(bf16[256,384]{0,1:T(8,128)(2,1)S(1)} %get-tuple-element.411), channel_id=1, source_target_pairs={{0,1},{1,2},{2,3},{3,4},{4,5},{5,6},{6,7},{7,8},{8,9},{9,10},{10,1... | collective-permute-start | bytes 589832 | tf_op jit(solution)/shard_map/while/body/eval_jaxpr/ppermute | solution.py:18
  41.1 3.3 collective-permute-start.2
  41.2 8.5 %collective-permute-start.3 = (bf16[256,384]{0,1:T(8,128)(2,1)S(1)}, bf16[256,384]{0,1:T(8,128)(2,1)S(1)}, u32[]{:S(2)}, u32[]{:S(2)}) collective-permute-start(bf16[256,384]{0,1:T(8,128)(2,1)S(1)} %get-tuple-element.419), channel_id=1, source_target_pairs={{0,1},{1,2},{2,3},{3,4},{4,5},{5,6},{6,7},{7,8},{8,9},{9,10},{10,1... | collective-permute-start | bytes 589832 | tf_op jit(solution)/shard_map/while/body/eval_jaxpr/ppermute | solution.py:18
  52.5 21.9 %collective-permute-start.4 = (bf16[256,2048]{0,1:T(8,128)(2,1)}, bf16[256,2048]{0,1:T(8,128)(2,1)}, u32[]{:S(2)}, u32[]{:S(2)}) collective-permute-start(bf16[256,2048]{0,1:T(8,128)(2,1)} %bitcast.67), channel_id=1, source_target_pairs={{0,32},{32,64},{64,96},{96,128},{128,160},{160,192},{192,224},{1,3... | collective-permute-start | bytes 3145736 | tf_op jit(solution)/shard_map/while/body/eval_jaxpr/ppermute | solution.py:29
  77.9 3.4 collective-permute-start
  78.2 8.4 %collective-permute-start.1 = (bf16[256,384]{0,1:T(8,128)(2,1)S(1)}, bf16[256,384]{0,1:T(8,128)(2,1)S(1)}, u32[]{:S(2)}, u32[]{:S(2)}) collective-permute-start(bf16[256,384]{0,1:T(8,128)(2,1)S(1)} %get-tuple-element.411), channel_id=1, source_target_pairs={{0,1},{1,2},{2,3},{3,4},{4,5},{5,6},{6,7},{7,8},{8,9},{9,10},{10,1... | collective-permute-start | bytes 589832 | tf_op jit(solution)/shard_map/while/body/eval_jaxpr/ppermute | solution.py:18
  88.4 3.3 collective-permute-start.2
  88.5 8.5 %collective-permute-start.3 = (bf16[256,384]{0,1:T(8,128)(2,1)S(1)}, bf16[256,384]{0,1:T(8,128)(2,1)S(1)}, u32[]{:S(2)}, u32[]{:S(2)}) collective-permute-start(bf16[256,384]{0,1:T(8,128)(2,1)S(1)} %get-tuple-element.419), channel_id=1, source_target_pairs={{0,1},{1,2},{2,3},{3,4},{4,5},{5,6},{6,7},{7,8},{8,9},{9,10},{10,1... | collective-permute-start | bytes 589832 | tf_op jit(solution)/shard_map/while/body/eval_jaxpr/ppermute | solution.py:18
  99.7 21.9 %collective-permute-start.4 = (bf16[256,2048]{0,1:T(8,128)(2,1)}, bf16[256,2048]{0,1:T(8,128)(2,1)}, u32[]{:S(2)}, u32[]{:S(2)}) collective-permute-start(bf16[256,2048]{0,1:T(8,128)(2,1)} %bitcast.67), channel_id=1, source_target_pairs={{0,32},{32,64},{64,96},{96,128},{128,160},{160,192},{192,224},{1,3... | collective-permute-start | bytes 3145736 | tf_op jit(solution)/shard_map/while/body/eval_jaxpr/ppermute | solution.py:29
  125.2 3.4 collective-permute-start
  125.3 8.5 %collective-permute-start.1 = (bf16[256,384]{0,1:T(8,128)(2,1)S(1)}, bf16[256,384]{0,1:T(8,128)(2,1)S(1)}, u32[]{:S(2)}, u32[]{:S(2)}) collective-permute-start(bf16[256,384]{0,1:T(8,128)(2,1)S(1)} %get-tuple-element.411), channel_id=1, source_target_pairs={{0,1},{1,2},{2,3},{3,4},{4,5},{5,6},{6,7},{7,8},{8,9},{9,10},{10,1... | collective-permute-start | bytes 589832 | tf_op jit(solution)/shard_map/while/body/eval_jaxpr/ppermute | solution.py:18
  135.6 3.3 collective-permute-start.2
  135.6 8.5 %collective-permute-start.3 = (bf16[256,384]{0,1:T(8,128)(2,1)S(1)}, bf16[256,384]{0,1:T(8,128)(2,1)S(1)}, u32[]{:S(2)}, u32[]{:S(2)}) collective-permute-start(bf16[256,384]{0,1:T(8,128)(2,1)S(1)} %get-tuple-element.419), channel_id=1, source_target_pairs={{0,1},{1,2},{2,3},{3,4},{4,5},{5,6},{6,7},{7,8},{8,9},{9,10},{10,1... | collective-permute-start | bytes 589832 | tf_op jit(solution)/shard_map/while/body/eval_jaxpr/ppermute | solution.py:18
  146.9 21.9 %collective-permute-start.4 = (bf16[256,2048]{0,1:T(8,128)(2,1)}, bf16[256,2048]{0,1:T(8,128)(2,1)}, u32[]{:S(2)}, u32[]{:S(2)}) collective-permute-start(bf16[256,2048]{0,1:T(8,128)(2,1)} %bitcast.67), channel_id=1, source_target_pairs={{0,32},{32,64},{64,96},{96,128},{128,160},{160,192},{192,224},{1,3... | collective-permute-start | bytes 3145736 | tf_op jit(solution)/shard_map/while/body/eval_jaxpr/ppermute | solution.py:29
  172.4 3.4 collective-permute-start
  172.5 8.5 %collective-permute-start.1 = (bf16[256,384]{0,1:T(8,128)(2,1)S(1)}, bf16[256,384]{0,1:T(8,128)(2,1)S(1)}, u32[]{:S(2)}, u32[]{:S(2)}) collective-permute-start(bf16[256,384]{0,1:T(8,128)(2,1)S(1)} %get-tuple-element.411), channel_id=1, source_target_pairs={{0,1},{1,2},{2,3},{3,4},{4,5},{5,6},{6,7},{7,8},{8,9},{9,10},{10,1... | collective-permute-start | bytes 589832 | tf_op jit(solution)/shard_map/while/body/eval_jaxpr/ppermute | solution.py:18
  182.7 3.3 collective-permute-start.2
  182.8 8.5 %collective-permute-start.3 = (bf16[256,384]{0,1:T(8,128)(2,1)S(1)}, bf16[256,384]{0,1:T(8,128)(2,1)S(1)}, u32[]{:S(2)}, u32[]{:S(2)}) collective-permute-start(bf16[256,384]{0,1:T(8,128)(2,1)S(1)} %get-tuple-element.419), channel_id=1, source_target_pairs={{0,1},{1,2},{2,3},{3,4},{4,5},{5,6},{6,7},{7,8},{8,9},{9,10},{10,1... | collective-permute-start | bytes 589832 | tf_op jit(solution)/shard_map/while/body/eval_jaxpr/ppermute | solution.py:18
  194.1 21.9 %collective-permute-start.4 = (bf16[256,2048]{0,1:T(8,128)(2,1)}, bf16[256,2048]{0,1:T(8,128)(2,1)}, u32[]{:S(2)}, u32[]{:S(2)}) collective-permute-start(bf16[256,2048]{0,1:T(8,128)(2,1)} %bitcast.67), channel_id=1, source_target_pairs={{0,32},{32,64},{64,96},{96,128},{128,160},{160,192},{192,224},{1,3... | collective-permute-start | bytes 3145736 | tf_op jit(solution)/shard_map/while/body/eval_jaxpr/ppermute | solution.py:29
  219.5 3.4 collective-permute-start
  219.6 8.5 %collective-permute-start.1 = (bf16[256,384]{0,1:T(8,128)(2,1)S(1)}, bf16[256,384]{0,1:T(8,128)(2,1)S(1)}, u32[]{:S(2)}, u32[]{:S(2)}) collective-permute-start(bf16[256,384]{0,1:T(8,128)(2,1)S(1)} %get-tuple-element.411), channel_id=1, source_target_pairs={{0,1},{1,2},{2,3},{3,4},{4,5},{5,6},{6,7},{7,8},{8,9},{9,10},{10,1... | collective-permute-start | bytes 589832 | tf_op jit(solution)/shard_map/while/body/eval_jaxpr/ppermute | solution.py:18
  229.9 3.3 collective-permute-start.2
  230.0 8.5 %collective-permute-start.3 = (bf16[256,384]{0,1:T(8,128)(2,1)S(1)}, bf16[256,384]{0,1:T(8,128)(2,1)S(1)}, u32[]{:S(2)}, u32[]{:S(2)}) collective-permute-start(bf16[256,384]{0,1:T(8,128)(2,1)S(1)} %get-tuple-element.419), channel_id=1, source_target_pairs={{0,1},{1,2},{2,3},{3,4},{4,5},{5,6},{6,7},{7,8},{8,9},{9,10},{10,1... | collective-permute-start | bytes 589832 | tf_op jit(solution)/shard_map/while/body/eval_jaxpr/ppermute | solution.py:18
  241.2 22.1 %collective-permute-start.4 = (bf16[256,2048]{0,1:T(8,128)(2,1)}, bf16[256,2048]{0,1:T(8,128)(2,1)}, u32[]{:S(2)}, u32[]{:S(2)}) collective-permute-start(bf16[256,2048]{0,1:T(8,128)(2,1)} %bitcast.67), channel_id=1, source_target_pairs={{0,32},{32,64},{64,96},{96,128},{128,160},{160,192},{192,224},{1,3... | collective-permute-start | bytes 3145736 | tf_op jit(solution)/shard_map/while/body/eval_jaxpr/ppermute | solution.py:29
  266.9 3.4 collective-permute-start
  267.0 8.5 %collective-permute-start.1 = (bf16[256,384]{0,1:T(8,128)(2,1)S(1)}, bf16[256,384]{0,1:T(8,128)(2,1)S(1)}, u32[]{:S(2)}, u32[]{:S(2)}) collective-permute-start(bf16[256,384]{0,1:T(8,128)(2,1)S(1)} %get-tuple-element.411), channel_id=1, source_target_pairs={{0,1},{1,2},{2,3},{3,4},{4,5},{5,6},{6,7},{7,8},{8,9},{9,10},{10,1... | collective-permute-start | bytes 589832 | tf_op jit(solution)/shard_map/while/body/eval_jaxpr/ppermute | solution.py:18
  277.3 3.3 collective-permute-start.2
  277.4 8.5 %collective-permute-start.3 = (bf16[256,384]{0,1:T(8,128)(2,1)S(1)}, bf16[256,384]{0,1:T(8,128)(2,1)S(1)}, u32[]{:S(2)}, u32[]{:S(2)}) collective-permute-start(bf16[256,384]{0,1:T(8,128)(2,1)S(1)} %get-tuple-element.419), channel_id=1, source_target_pairs={{0,1},{1,2},{2,3},{3,4},{4,5},{5,6},{6,7},{7,8},{8,9},{9,10},{10,1... | collective-permute-start | bytes 589832 | tf_op jit(solution)/shard_map/while/body/eval_jaxpr/ppermute | solution.py:18
  288.6 23.1 %collective-permute-start.4 = (bf16[256,2048]{0,1:T(8,128)(2,1)}, bf16[256,2048]{0,1:T(8,128)(2,1)}, u32[]{:S(2)}, u32[]{:S(2)}) collective-permute-start(bf16[256,2048]{0,1:T(8,128)(2,1)} %bitcast.67), channel_id=1, source_target_pairs={{0,32},{32,64},{64,96},{96,128},{128,160},{160,192},{192,224},{1,3... | collective-permute-start | bytes 3145736 | tf_op jit(solution)/shard_map/while/body/eval_jaxpr/ppermute | solution.py:29
  315.3 3.4 collective-permute-start
  315.4 8.5 %collective-permute-start.1 = (bf16[256,384]{0,1:T(8,128)(2,1)S(1)}, bf16[256,384]{0,1:T(8,128)(2,1)S(1)}, u32[]{:S(2)}, u32[]{:S(2)}) collective-permute-start(bf16[256,384]{0,1:T(8,128)(2,1)S(1)} %get-tuple-element.411), channel_id=1, source_target_pairs={{0,1},{1,2},{2,3},{3,4},{4,5},{5,6},{6,7},{7,8},{8,9},{9,10},{10,1... | collective-permute-start | bytes 589832 | tf_op jit(solution)/shard_map/while/body/eval_jaxpr/ppermute | solution.py:18
  325.7 3.3 collective-permute-start.2
  325.8 8.5 %collective-permute-start.3 = (bf16[256,384]{0,1:T(8,128)(2,1)S(1)}, bf16[256,384]{0,1:T(8,128)(2,1)S(1)}, u32[]{:S(2)}, u32[]{:S(2)}) collective-permute-start(bf16[256,384]{0,1:T(8,128)(2,1)S(1)} %get-tuple-element.419), channel_id=1, source_target_pairs={{0,1},{1,2},{2,3},{3,4},{4,5},{5,6},{6,7},{7,8},{8,9},{9,10},{10,1... | collective-permute-start | bytes 589832 | tf_op jit(solution)/shard_map/while/body/eval_jaxpr/ppermute | solution.py:18
  337.0 23.1 %collective-permute-start.4 = (bf16[256,2048]{0,1:T(8,128)(2,1)}, bf16[256,2048]{0,1:T(8,128)(2,1)}, u32[]{:S(2)}, u32[]{:S(2)}) collective-permute-start(bf16[256,2048]{0,1:T(8,128)(2,1)} %bitcast.67), channel_id=1, source_target_pairs={{0,32},{32,64},{64,96},{96,128},{128,160},{160,192},{192,224},{1,3... | collective-permute-start | bytes 3145736 | tf_op jit(solution)/shard_map/while/body/eval_jaxpr/ppermute | solution.py:29
  363.7 3.4 collective-permute-start
  363.8 8.5 %collective-permute-start.1 = (bf16[256,384]{0,1:T(8,128)(2,1)S(1)}, bf16[256,384]{0,1:T(8,128)(2,1)S(1)}, u32[]{:S(2)}, u32[]{:S(2)}) collective-permute-start(bf16[256,384]{0,1:T(8,128)(2,1)S(1)} %get-tuple-element.411), channel_id=1, source_target_pairs={{0,1},{1,2},{2,3},{3,4},{4,5},{5,6},{6,7},{7,8},{8,9},{9,10},{10,1... | collective-permute-start | bytes 589832 | tf_op jit(solution)/shard_map/while/body/eval_jaxpr/ppermute | solution.py:18
  374.1 3.3 collective-permute-start.2
  374.2 8.5 %collective-permute-start.3 = (bf16[256,384]{0,1:T(8,128)(2,1)S(1)}, bf16[256,384]{0,1:T(8,128)(2,1)S(1)}, u32[]{:S(2)}, u32[]{:S(2)}) collective-permute-start(bf16[256,384]{0,1:T(8,128)(2,1)S(1)} %get-tuple-element.419), channel_id=1, source_target_pairs={{0,1},{1,2},{2,3},{3,4},{4,5},{5,6},{6,7},{7,8},{8,9},{9,10},{10,1... | collective-permute-start | bytes 589832 | tf_op jit(solution)/shard_map/while/body/eval_jaxpr/ppermute | solution.py:18
  385.4 23.1 %collective-permute-start.4 = (bf16[256,2048]{0,1:T(8,128)(2,1)}, bf16[256,2048]{0,1:T(8,128)(2,1)}, u32[]{:S(2)}, u32[]{:S(2)}) collective-permute-start(bf16[256,2048]{0,1:T(8,128)(2,1)} %bitcast.67), channel_id=1, source_target_pairs={{0,32},{32,64},{64,96},{96,128},{128,160},{160,192},{192,224},{1,3... | collective-permute-start | bytes 3145736 | tf_op jit(solution)/shard_map/while/body/eval_jaxpr/ppermute | solution.py:29
  412.1 3.4 collective-permute-start
  412.2 8.5 %collective-permute-start.1 = (bf16[256,384]{0,1:T(8,128)(2,1)S(1)}, bf16[256,384]{0,1:T(8,128)(2,1)S(1)}, u32[]{:S(2)}, u32[]{:S(2)}) collective-permute-start(bf16[256,384]{0,1:T(8,128)(2,1)S(1)} %get-tuple-element.411), channel_id=1, source_target_pairs={{0,1},{1,2},{2,3},{3,4},{4,5},{5,6},{6,7},{7,8},{8,9},{9,10},{10,1... | collective-permute-start | bytes 589832 | tf_op jit(solution)/shard_map/while/body/eval_jaxpr/ppermute | solution.py:18
  422.5 3.3 collective-permute-start.2
  422.5 8.5 %collective-permute-start.3 = (bf16[256,384]{0,1:T(8,128)(2,1)S(1)}, bf16[256,384]{0,1:T(8,128)(2,1)S(1)}, u32[]{:S(2)}, u32[]{:S(2)}) collective-permute-start(bf16[256,384]{0,1:T(8,128)(2,1)S(1)} %get-tuple-element.419), channel_id=1, source_target_pairs={{0,1},{1,2},{2,3},{3,4},{4,5},{5,6},{6,7},{7,8},{8,9},{9,10},{10,1... | collective-permute-start | bytes 589832 | tf_op jit(solution)/shard_map/while/body/eval_jaxpr/ppermute | solution.py:18
  433.8 23.1 %collective-permute-start.4 = (bf16[256,2048]{0,1:T(8,128)(2,1)}, bf16[256,2048]{0,1:T(8,128)(2,1)}, u32[]{:S(2)}, u32[]{:S(2)}) collective-permute-start(bf16[256,2048]{0,1:T(8,128)(2,1)} %bitcast.67), channel_id=1, source_target_pairs={{0,32},{32,64},{64,96},{96,128},{128,160},{160,192},{192,224},{1,3... | collective-permute-start | bytes 3145736 | tf_op jit(solution)/shard_map/while/body/eval_jaxpr/ppermute | solution.py:29
Sparse Core Ops, SparseCore 0:
  460.1 80.2 all-reduce.1
where the time goes:
time: 554 us; the launch traced here: 549 us
  waiting for transfers between devices  366 us (66%)
  local copies, waits for them, and re-layouts  78.2 us (14%)
  matrix products  34.4 us (6%)
  starting transfers between devices  26.1 us (5%)
  other arithmetic  25.8 us (5%)
  between operations  17.3 us (3%)
    ppermute x9, waiting for transfers between devices, from_behind(): lax.ppermute(value, axis, [(source, source + steps) for source in range(f...  167 us
    ppermute x18, waiting for transfers between devices, padded(): lax.ppermute(lax.slice_in_dim(block, block.shape[dim] - width, None, axis...  94.1 us
    psum x1, waiting for transfers between devices, spread(): return lax.psum(kept, axis)  80.5 us
    dot_general x54, matrix products, apply_layer(): jnp.einsum('rjk,jkn->rjn', shifted, block_weights, preferred_element_type...  34.4 us
    ppermute x18, waiting for transfers between devices, padded(): lax.ppermute(lax.slice_in_dim(block, 0, width, axis=dim), axis, backward)  24.5 us
    squeeze x9, local copies, waits for them, and re-layouts, apply_layer(): layer_weights = table[layer, first:first + out_blocks]  22.4 us
    dynamic_slice x18, local copies, waits for them, and re-layouts, advance(): lax.dynamic_index_in_dim(finished_rows, slot_index, 0, keepdims=False)  19.8 us
    dynamic_update_slice x18, local copies, waits for them, and re-layouts, advance(): lax.dynamic_update_index_in_dim(finished_rows, jnp.where(finished, produc...  15.2 us
  transfers between devices with their start and end apart: 46, of which 38 were waited for; matrix products, arithmetic and copies ran while one was open for 9% of the time, Pallas kernels for 0%

commit v1 on v0

v1 whole, which is shorter than its diff:
```python
import functools

import jax
import jax.numpy as jnp
from jax import lax
from jax.experimental import pallas as pl
from jax.experimental.pallas import tpu as pltpu
from jax.sharding import PartitionSpec as P

MESH = pl.DeviceIdType.MESH
HALO = 3
ceiling = 2.0
ROWS = 16
AHEAD = 2


def kernel(
    dims, offs, x, w, bias, out,
    wa, wb, bl, br, bs, zin, zout, hl, hr, work, mid,
    zs, zr, ls, lr, rs, rr, og, ws, wr,
):
    sections, devices, micro, share, chunks, blocks, size = dims
    rows = ROWS
    width = 2 * HALO * size
    sec = lax.axis_index("section")
    me = lax.axis_index("neuron")
    left = lax.rem(me + devices - 1, devices)
    right = lax.rem(me + 1, devices)
    after = lax.rem(sec + 1, sections)
    before = lax.rem(sec + sections - 1, sections)
    per_share = share // rows
    per_owner = micro * per_share

    barrier = pltpu.get_barrier_semaphore()
    for where in ({"neuron": left}, {"neuron": right}, {"section": after}, {"section": before}):
        pl.semaphore_signal(barrier, inc=1, device_id=where, device_id_type=MESH)

    def place(c):
        owner = c // per_owner
        slot = c % per_owner
        batch = slot // per_share
        row = (slot % per_share) * rows
        return owner, slot, batch, row

    def fetch(c):
        owner, _, batch, row = place(c)
        start = pl.multiple_of(owner * share + row, rows)
        return pltpu.make_async_copy(x.at[batch, pl.ds(start, rows), :], zin.at[c], zr.at[c])

    def forward(c):
        return pltpu.make_async_remote_copy(
            src_ref=zout.at[c], dst_ref=zin.at[c], send_sem=zs.at[c], recv_sem=zr.at[c],
            device_id={"section": after}, device_id_type=MESH)

    def deliver(c):
        owner, slot, batch, row = place(c)
        target = out.at[batch, pl.ds(pl.multiple_of(row, rows), rows), :]
        return pltpu.make_async_remote_copy(
            src_ref=zout.at[c], dst_ref=target, send_sem=zs.at[c], recv_sem=og.at[slot],
            device_id={"section": owner}, device_id_type=MESH)

    def keep(c):
        _, _, batch, row = place(c)
        target = out.at[batch, pl.ds(pl.multiple_of(row, rows), rows), :]
        return pltpu.make_async_copy(zout.at[c], target, zs.at[c])

    def to_left(c):
        return pltpu.make_async_remote_copy(
            src_ref=zin.at[c, :, pl.ds(0, width)], dst_ref=hr.at[c], send_sem=ls.at[c], recv_sem=rr.at[c],
            device_id={"neuron": left}, device_id_type=MESH)

    def to_right(c):
        return pltpu.make_async_remote_copy(
            src_ref=zin.at[c, :, pl.ds(blocks * size - width, width)], dst_ref=hl.at[c],
            send_sem=rs.at[c], recv_sem=lr.at[c],
            device_id={"neuron": right}, device_id_type=MESH)

    first = sec == 0
    last = sec == sections - 1

    @pl.when(first)
    def _():
        @pl.loop(0, chunks)
        def _(c):
            fetch(c).start()

    own_a = pltpu.make_async_copy(w.at[0], wa.at[pl.ds(HALO, blocks)], ws.at[0])
    own_b = pltpu.make_async_copy(w.at[1], wb, ws.at[1])
    own_a.start()
    own_b.start()
    pl.semaphore_wait(barrier, 4)

    def receive(c):
        @pl.when(first)
        def _():
            fetch(c).wait()

        @pl.when(jnp.logical_not(first))
        def _():
            forward(c).wait_recv()

        to_left(c).start()
        to_right(c).start()

    edge_left = pltpu.make_async_remote_copy(
        src_ref=w.at[0, pl.ds(0, HALO)], dst_ref=wa.at[pl.ds(HALO + blocks, HALO)],
        send_sem=ws.at[2], recv_sem=wr.at[0], device_id={"neuron": left}, device_id_type=MESH)
    edge_right = pltpu.make_async_remote_copy(
        src_ref=w.at[0, pl.ds(blocks - HALO, HALO)], dst_ref=wa.at[pl.ds(0, HALO)],
        send_sem=ws.at[3], recv_sem=wr.at[1], device_id={"neuron": right}, device_id_type=MESH)
    bias_left = pltpu.make_async_remote_copy(
        src_ref=bias.at[:, pl.ds(0, HALO * size)], dst_ref=br,
        send_sem=ws.at[4], recv_sem=wr.at[2], device_id={"neuron": left}, device_id_type=MESH)
    bias_right = pltpu.make_async_remote_copy(
        src_ref=bias.at[:, pl.ds((blocks - HALO) * size, HALO * size)], dst_ref=bl,
        send_sem=ws.at[5], recv_sem=wr.at[3], device_id={"neuron": right}, device_id_type=MESH)
    edges = (bias_left, bias_right, edge_left, edge_right)
    for copy in edges:
        copy.start()
    for c in range(AHEAD):
        @pl.when(first)
        def _(c=c):
            receive(c)
    for copy in (bias_left, bias_right):
        copy.wait()
    span = blocks + 2 * HALO
    own = bias[...].astype(jnp.float32)
    from_left = bl[...].astype(jnp.float32)
    from_right = br[...].astype(jnp.float32)
    for j in range(HALO):
        bs[j : j + 1, :] = from_left[0:1, j * size : (j + 1) * size]
        bs[HALO + blocks + j : HALO + blocks + j + 1, :] = from_right[0:1, j * size : (j + 1) * size]
    for j in range(blocks):
        bs[HALO + j : HALO + j + 1, :] = own[0:1, j * size : (j + 1) * size]
        bs[span + j : span + j + 1, :] = own[1:2, j * size : (j + 1) * size]
    own_a.wait()
    own_b.wait()
    edge_left.wait()
    edge_right.wait()
    for c in range(AHEAD):
        @pl.when(jnp.logical_not(first))
        def _(c=c):
            receive(c)

    def apply(source, weights, j, shift, bias_row):
        taken = [source[j + s] for s in shift]
        joined = jnp.concatenate(taken, axis=1)
        total = jnp.dot(joined, weights[j].reshape(len(shift) * size, size), preferred_element_type=jnp.float32)
        total = total + bs[bias_row : bias_row + 1, :]
        return jnp.minimum(jnp.maximum(total, 0.0), ceiling).astype(jnp.bfloat16)

    bands = w.shape[2]
    shift_a = [offs[0, b] + HALO for b in range(bands)]
    shift_b = [offs[1, b] + HALO for b in range(bands)]

    @pl.loop(0, chunks)
    def _(c):
        @pl.when(c + AHEAD < chunks)
        def _():
            receive(c + AHEAD)

        for j in range(blocks):
            work[2 * HALO + j] = zin[c, :, j * size : (j + 1) * size]
        to_left(c).wait_recv()
        for j in range(2 * HALO):
            work[2 * HALO + blocks + j] = hr[c, :, j * size : (j + 1) * size]
        to_right(c).wait_recv()
        for j in range(2 * HALO):
            work[j] = hl[c, :, j * size : (j + 1) * size]
        for j in range(span):
            mid[j] = apply(work, wa, j, shift_a, j)
        for j in range(blocks):
            zout[c, :, j * size : (j + 1) * size] = apply(mid, wb, j, shift_b, span + j)

        @pl.when(jnp.logical_not(last))
        def _():
            forward(c).start()

        @pl.when(last)
        def _():
            @pl.when(c // per_owner < sections - 1)
            def _():
                deliver(c).start()

            @pl.when(c // per_owner == sections - 1)
            def _():
                keep(c).start()

    @pl.loop(0, chunks)
    def _(c):
        to_left(c).wait_send()
        to_right(c).wait_send()

        @pl.when(jnp.logical_not(last))
        def _():
            forward(c).wait_send()

        @pl.when(last)
        def _():
            @pl.when(c // per_owner < sections - 1)
            def _():
                deliver(c).wait_send()

            @pl.when(c // per_owner == sections - 1)
            def _():
                keep(c).wait()

    @pl.when(jnp.logical_not(last))
    def _():
        @pl.loop(0, per_owner)
        def _(c):
            deliver(c).wait_recv()


def shards(sections, devices, inputs, weights, bias, offsets):
    micro, row_count, local = inputs.shape
    layers, blocks, bands, size = weights.shape[:4]
    share = row_count // sections
    chunks = micro * row_count // ROWS
    span = blocks + 2 * HALO
    bf16, dma = jnp.bfloat16, pltpu.SemaphoreType.DMA
    dims = (sections, devices, micro, share, chunks, blocks, size)
    return pl.pallas_call(
        functools.partial(kernel, dims),
        out_shape=jax.ShapeDtypeStruct((micro, share, local), bf16),
        in_specs=[
            pl.BlockSpec(memory_space=pltpu.SMEM),
            pl.BlockSpec(memory_space=pl.ANY),
            pl.BlockSpec(memory_space=pl.ANY),
            pl.BlockSpec(memory_space=pltpu.VMEM),
        ],
        out_specs=pl.BlockSpec(memory_space=pl.ANY),
        scratch_shapes=[
            pltpu.VMEM((span, bands, size, size), bf16),
            pltpu.VMEM((blocks, bands, size, size), bf16),
            pltpu.VMEM((layers, HALO * size), bf16),
            pltpu.VMEM((layers, HALO * size), bf16),
            pltpu.VMEM((span + blocks + 2, size), jnp.float32),
            pltpu.VMEM((chunks, ROWS, local), bf16),
            pltpu.VMEM((chunks, ROWS, local), bf16),
            pltpu.VMEM((chunks, ROWS, 2 * HALO * size), bf16),
            pltpu.VMEM((chunks, ROWS, 2 * HALO * size), bf16),
            pltpu.VMEM((span + 2 * HALO, ROWS, size), bf16),
            pltpu.VMEM((span, ROWS, size), bf16),
            dma((chunks,)), dma((chunks,)), dma((chunks,)), dma((chunks,)), dma((chunks,)), dma((chunks,)),
            dma((micro * share // ROWS,)), dma((6,)), dma((4,)),
        ],
        compiler_params=pltpu.CompilerParams(collective_id=0, has_side_effects=True),
    )(offsets, inputs, weights, bias)


def solution(mesh):
    in_specs = (
        P(None, None, "neuron"),
        P("section", "neuron", None, None, None),
        P("section", "neuron"),
        P("section", None),
    )
    out_specs = P(None, "section", "neuron")
    body = functools.partial(shards, mesh.shape["section"], mesh.shape["neuron"])
    return jax.shard_map(body, mesh=mesh, in_specs=in_specs, out_specs=out_specs, check_vma=False)
```

time: 554 us -> 128 us (0.23)
  waiting for transfers between devices: 366 us -> 0 us
  Pallas kernels: 0 us -> 127 us
  local copies, waits for them, and re-layouts: 78.2 us -> 1.67 us
  matrix products: 34.4 us -> 0 us
  starting transfers between devices: 26.1 us -> 0 us
  other arithmetic: 25.8 us -> 0 us
  between operations: 17.3 us -> 0.01 us
    ppermute x45 -> x0, waiting for transfers between devices: 285 us -> none  [the longest x9 167 us: from_behind(): lax.ppermute(value, axis, [(source, source + steps) for source in range(f...]
    pallas_call x0 -> x1, Pallas kernels: none -> 127 us  [shards(): pl.pallas_call(functools.partial(kernel, dims), out_shape=jax.ShapeDtypeS...]
    psum x1 -> x0, waiting for transfers between devices: 80.5 us -> none  [spread(): return lax.psum(kept, axis)]
    dot_general x54 -> x0, matrix products: 34.4 us -> none  [apply_layer(): jnp.einsum('rjk,jkn->rjn', shifted, block_weights, preferred_element_type...]
    dynamic_slice x46 -> x0, local copies, waits for them, and re-layouts: 30.1 us -> none  [the longest x18 19.8 us: advance(): lax.dynamic_index_in_dim(finished_rows, slot_index, 0, keepdims=False)]
    ppermute x45 -> x0, starting transfers between devices: 26.1 us -> none  [the longest x9 11.5 us: from_behind(): lax.ppermute(value, axis, [(source, source + steps) for source in range(f...]
    squeeze x9 -> x0, local copies, waits for them, and re-layouts: 22.4 us -> none  [apply_layer(): layer_weights = table[layer, first:first + out_blocks]]
    select_n x19 -> x0, other arithmetic: 18.7 us -> none  [the longest x9 12.1 us: advance(): current = jnp.where(section_index == 0, arriving, incoming)]
  transfers between devices with their start and end apart: 46 -> 0, of which waited for: 38 -> 0; matrix products, arithmetic and copies ran while one was open for 9% -> 0% of each run, Pallas kernels for 0% -> 0%
where the time goes in v1:
time: 128 us
  Pallas kernels  127 us (99%)
  local copies, waits for them, and re-layouts  1.67 us (1%)
    pallas_call x1, Pallas kernels, shards(): pl.pallas_call(functools.partial(kernel, dims), out_shape=jax.ShapeDtypeS...  127 us

profile of v1, /device:TPU:224, one launch (start us, length us, event | category | flops | bytes accessed | tf_op | source)
XLA Modules:
  0.0 128.3 jit_solution(13349139706765521289)
XLA Ops:
  0.0 126.7 %shard_map.46 = bf16[2,32,2048]{2,1,0:T(8,128)(2,1)} custom-call(s32[2,3]{1,0:T(2,128)} %offs.1, bf16[2,256,2048]{2,1,0:T(8,128)(2,1)} %x.1, bf16[2,16,3,128,128]{4,3,2,1,0:T(8,128)(2,1)} %w.1, bf16[2,2048]{1,0:T(2,128)(2,1)} %bias.1), custom_call_target="tpu_custom_call" | custom-call | tf_op jit(solution)/shard_map/pallas_call | solution.py:223
  126.7 1.7 %copy.6 = bf16[2,32,2048]{2,1,0:T(8,128)(2,1)} copy(bf16[2,32,2048]{2,1,0:T(8,128)(2,1)} %shard_map.46) | data formatting | bytes 524288

commit v2 on v1

--- a/solution.py
+++ b/solution.py
@@ -11,12 +11,12 @@
 HALO = 3
 ceiling = 2.0
 ROWS = 16
-AHEAD = 2
+AHEAD = 3
 
 
 def kernel(
     dims, offs, x, w, bias, out,
-    wa, wb, bl, br, bs, zin, zout, hl, hr, work, mid,
+    wa, wb, bl, br, bs, zin, zout, hl, hr, work, mid_low, mid_high,
     zs, zr, ls, lr, rs, rr, og, ws, wr,
 ):
     sections, devices, micro, share, chunks, blocks, size = dims
@@ -32,8 +32,18 @@
     per_owner = micro * per_share
 
     barrier = pltpu.get_barrier_semaphore()
-    for where in ({"neuron": left}, {"neuron": right}, {"section": after}, {"section": before}):
+    first = sec == 0
+    last = sec == sections - 1
+    for where in ({"neuron": left}, {"neuron": right}):
         pl.semaphore_signal(barrier, inc=1, device_id=where, device_id_type=MESH)
+
+    @pl.when(jnp.logical_not(last))
+    def _():
+        pl.semaphore_signal(barrier, inc=1, device_id={"section": after}, device_id_type=MESH)
+
+    @pl.when(jnp.logical_not(first))
+    def _():
+        pl.semaphore_signal(barrier, inc=1, device_id={"section": before}, device_id_type=MESH)
 
     def place(c):
         owner = c // per_owner
@@ -75,20 +85,30 @@
             send_sem=rs.at[c], recv_sem=lr.at[c],
             device_id={"neuron": right}, device_id_type=MESH)
 
-    first = sec == 0
-    last = sec == sections - 1
-
     @pl.when(first)
     def _():
-        @pl.loop(0, chunks)
-        def _(c):
+        for c in range(AHEAD):
             fetch(c).start()
 
     own_a = pltpu.make_async_copy(w.at[0], wa.at[pl.ds(HALO, blocks)], ws.at[0])
     own_b = pltpu.make_async_copy(w.at[1], wb, ws.at[1])
     own_a.start()
     own_b.start()
-    pl.semaphore_wait(barrier, 4)
+
+    @pl.when(first)
+    def _():
+        @pl.loop(AHEAD, chunks)
+        def _(c):
+            fetch(c).start()
+
+    @pl.when(jnp.logical_or(first, last))
+    def _():
+        pl.semaphore_wait(barrier, 3)
+
+    @pl.when(jnp.logical_not(jnp.logical_or(first, last)))
+    def _():
+        pl.semaphore_wait(barrier, 4)
+
 
     def receive(c):
         @pl.when(first)
@@ -142,12 +162,27 @@
         def _(c=c):
             receive(c)
 
-    def apply(source, weights, j, shift, bias_row):
-        taken = [source[j + s] for s in shift]
-        joined = jnp.concatenate(taken, axis=1)
-        total = jnp.dot(joined, weights[j].reshape(len(shift) * size, size), preferred_element_type=jnp.float32)
-        total = total + bs[bias_row : bias_row + 1, :]
-        return jnp.minimum(jnp.maximum(total, 0.0), ceiling).astype(jnp.bfloat16)
+    def apply(source, weights, j, at, shift, bias_row):
+        low = [jnp.concatenate([source[at + k + s] for s in shift[:2]], axis=1) for k in range(2)]
+        sums = [
+            jnp.dot(low[k], weights[j + k, 0:2].reshape(2 * size, size), preferred_element_type=jnp.float32)
+            for k in range(2)
+        ]
+        zero = jnp.zeros((rows, size), jnp.bfloat16)
+        third = jnp.concatenate(
+            [
+                jnp.concatenate([source[at + shift[2]], zero], axis=1),
+                jnp.concatenate([zero, source[at + 1 + shift[2]]], axis=1),
+            ],
+            axis=0,
+        )
+        both = jnp.concatenate([weights[j, 2], weights[j + 1, 2]], axis=0)
+        rest = jnp.dot(third, both, preferred_element_type=jnp.float32)
+        done = []
+        for k in range(2):
+            total = sums[k] + rest[k * rows : (k + 1) * rows] + bs[bias_row + k : bias_row + k + 1, :]
+            done.append(jnp.minimum(jnp.maximum(total, 0.0), ceiling).astype(jnp.bfloat16))
+        return done
 
     bands = w.shape[2]
     shift_a = [offs[0, b] + HALO for b in range(bands)]
@@ -167,10 +202,17 @@
         to_right(c).wait_recv()
         for j in range(2 * HALO):
             work[j] = hl[c, :, j * size : (j + 1) * size]
-        for j in range(span):
-            mid[j] = apply(work, wa, j, shift_a, j)
-        for j in range(blocks):
-            zout[c, :, j * size : (j + 1) * size] = apply(mid, wb, j, shift_b, span + j)
+        half = blocks // 2
+        for j in range(0, span, 2):
+            for k, block in enumerate(apply(work, wa, j, j, shift_a, j)):
+                if j + k < half + 2 * HALO:
+                    mid_low[j + k] = block
+                if j + k >= half:
+                    mid_high[j + k - half] = block
+        for j in range(0, blocks, 2):
+            source, at = (mid_low, j) if j < half else (mid_high, j - half)
+            for k, block in enumerate(apply(source, wb, j, at, shift_b, span + j)):
+                zout[c, :, (j + k) * size : (j + k + 1) * size] = block
 
         @pl.when(jnp.logical_not(last))
         def _():
@@ -241,7 +283,8 @@
             pltpu.VMEM((chunks, ROWS, 2 * HALO * size), bf16),
             pltpu.VMEM((chunks, ROWS, 2 * HALO * size), bf16),
             pltpu.VMEM((span + 2 * HALO, ROWS, size), bf16),
-            pltpu.VMEM((span, ROWS, size), bf16),
+            pltpu.VMEM((blocks // 2 + 2 * HALO, ROWS, size), bf16),
+            pltpu.VMEM((blocks // 2 + 2 * HALO, ROWS, size), bf16),
             dma((chunks,)), dma((chunks,)), dma((chunks,)), dma((chunks,)), dma((chunks,)), dma((chunks,)),
             dma((micro * share // ROWS,)), dma((6,)), dma((4,)),
         ],

time: 128 us -> 116 us (0.906)
  Pallas kernels: 127 us -> 114 us
    pallas_call x1, Pallas kernels: 127 us -> 114 us  [shards(): pl.pallas_call(functools.partial(kernel, dims), out_shape=jax.ShapeDtypeS...]
where the time goes in v2:
time: 116 us
  Pallas kernels  114 us (98%)
  local copies, waits for them, and re-layouts  1.67 us (1%)
    pallas_call x1, Pallas kernels, shards(): pl.pallas_call(functools.partial(kernel, dims), out_shape=jax.ShapeDtypeS...  114 us

profile of v2, /device:TPU:224, one launch (start us, length us, event | category | flops | bytes accessed | tf_op | source)
XLA Modules:
  0.0 115.7 jit_solution(13175238905088121004)
XLA Ops:
  0.0 114.0 %shard_map.46 = bf16[2,32,2048]{2,1,0:T(8,128)(2,1)} custom-call(s32[2,3]{1,0:T(2,128)} %offs.1, bf16[2,256,2048]{2,1,0:T(8,128)(2,1)} %x.1, bf16[2,16,3,128,128]{4,3,2,1,0:T(8,128)(2,1)} %w.1, bf16[2,2048]{1,0:T(2,128)(2,1)} %bias.1), custom_call_target="tpu_custom_call" | custom-call | tf_op jit(solution)/shard_map/pallas_call | solution.py:265
  114.0 1.7 %copy.6 = bf16[2,32,2048]{2,1,0:T(8,128)(2,1)} copy(bf16[2,32,2048]{2,1,0:T(8,128)(2,1)} %shard_map.46) | data formatting | bytes 524288

commit v3 on v2

--- a/solution.py
+++ b/solution.py
@@ -11,13 +11,14 @@
 HALO = 3
 ceiling = 2.0
 ROWS = 16
-AHEAD = 3
+OUTER = 3
+INNER = 2
 
 
 def kernel(
     dims, offs, x, w, bias, out,
-    wa, wb, bl, br, bs, zin, zout, hl, hr, work, mid_low, mid_high,
-    zs, zr, ls, lr, rs, rr, og, ws, wr,
+    wa, wb, bl, br, bs, zin, zout, ho, hi, work, mid_low, mid_high,
+    es, er, zs, zr, os, orr, ks, kr, og, ws, wr,
 ):
     sections, devices, micro, share, chunks, blocks, size = dims
     rows = ROWS
@@ -55,11 +56,26 @@
     def fetch(c):
         owner, _, batch, row = place(c)
         start = pl.multiple_of(owner * share + row, rows)
-        return pltpu.make_async_copy(x.at[batch, pl.ds(start, rows), :], zin.at[c], zr.at[c])
+        return pltpu.make_async_copy(x.at[batch, pl.ds(start, rows), :], zin.at[c], er.at[c])
+
+    odd = lax.rem(me, 2)
+    outer = lax.rem(me + devices - 1 + 2 * odd, devices)
+    inner = me + 1 - 2 * odd
+    rest = blocks * size - width
+    outer_start = pl.multiple_of(odd * rest, size)
+    inner_start = pl.multiple_of((1 - odd) * rest, size)
+    rest_start = pl.multiple_of((1 - odd) * width, size)
+
+    def forward_edge(c):
+        cut = pl.ds(outer_start, width)
+        return pltpu.make_async_remote_copy(
+            src_ref=zout.at[c, :, cut], dst_ref=zin.at[c, :, cut], send_sem=es.at[c], recv_sem=er.at[c],
+            device_id={"section": after}, device_id_type=MESH)
 
     def forward(c):
-        return pltpu.make_async_remote_copy(
-            src_ref=zout.at[c], dst_ref=zin.at[c], send_sem=zs.at[c], recv_sem=zr.at[c],
+        cut = pl.ds(rest_start, rest)
+        return pltpu.make_async_remote_copy(
+            src_ref=zout.at[c, :, cut], dst_ref=zin.at[c, :, cut], send_sem=zs.at[c], recv_sem=zr.at[c],
             device_id={"section": after}, device_id_type=MESH)
 
     def deliver(c):
@@ -74,20 +90,19 @@
         target = out.at[batch, pl.ds(pl.multiple_of(row, rows), rows), :]
         return pltpu.make_async_copy(zout.at[c], target, zs.at[c])
 
-    def to_left(c):
-        return pltpu.make_async_remote_copy(
-            src_ref=zin.at[c, :, pl.ds(0, width)], dst_ref=hr.at[c], send_sem=ls.at[c], recv_sem=rr.at[c],
-            device_id={"neuron": left}, device_id_type=MESH)
-
-    def to_right(c):
-        return pltpu.make_async_remote_copy(
-            src_ref=zin.at[c, :, pl.ds(blocks * size - width, width)], dst_ref=hl.at[c],
-            send_sem=rs.at[c], recv_sem=lr.at[c],
-            device_id={"neuron": right}, device_id_type=MESH)
+    def to_outer(c):
+        return pltpu.make_async_remote_copy(
+            src_ref=zin.at[c, :, pl.ds(outer_start, width)], dst_ref=ho.at[c], send_sem=os.at[c], recv_sem=orr.at[c],
+            device_id={"neuron": outer}, device_id_type=MESH)
+
+    def to_inner(c):
+        return pltpu.make_async_remote_copy(
+            src_ref=zin.at[c, :, pl.ds(inner_start, width)], dst_ref=hi.at[c], send_sem=ks.at[c], recv_sem=kr.at[c],
+            device_id={"neuron": inner}, device_id_type=MESH)
 
     @pl.when(first)
     def _():
-        for c in range(AHEAD):
+        for c in range(OUTER):
             fetch(c).start()
 
     own_a = pltpu.make_async_copy(w.at[0], wa.at[pl.ds(HALO, blocks)], ws.at[0])
@@ -97,7 +112,7 @@
 
     @pl.when(first)
     def _():
-        @pl.loop(AHEAD, chunks)
+        @pl.loop(OUTER, chunks)
         def _(c):
             fetch(c).start()
 
@@ -110,17 +125,29 @@
         pl.semaphore_wait(barrier, 4)
 
 
-    def receive(c):
+    def receive_outer(c):
         @pl.when(first)
         def _():
             fetch(c).wait()
 
         @pl.when(jnp.logical_not(first))
         def _():
+            forward_edge(c).wait_recv()
+
+        to_outer(c).start()
+
+    def receive_inner(c):
+        @pl.when(jnp.logical_not(first))
+        def _():
             forward(c).wait_recv()
 
-        to_left(c).start()
-        to_right(c).start()
+        to_inner(c).start()
+
+    def receive_first():
+        for c in range(OUTER):
+            receive_outer(c)
+            if c < INNER:
+                receive_inner(c)
 
     edge_left = pltpu.make_async_remote_copy(
         src_ref=w.at[0, pl.ds(0, HALO)], dst_ref=wa.at[pl.ds(HALO + blocks, HALO)],
@@ -137,10 +164,11 @@
     edges = (bias_left, bias_right, edge_left, edge_right)
     for copy in edges:
         copy.start()
-    for c in range(AHEAD):
-        @pl.when(first)
-        def _(c=c):
-            receive(c)
+
+    @pl.when(first)
+    def _():
+        receive_first()
+
     for copy in (bias_left, bias_right):
         copy.wait()
     span = blocks + 2 * HALO
@@ -157,10 +185,10 @@
     own_b.wait()
     edge_left.wait()
     edge_right.wait()
-    for c in range(AHEAD):
-        @pl.when(jnp.logical_not(first))
-        def _(c=c):
-            receive(c)
+
+    @pl.when(jnp.logical_not(first))
+    def _():
+        receive_first()
 
     def apply(source, weights, j, at, shift, bias_row):
         low = [jnp.concatenate([source[at + k + s] for s in shift[:2]], axis=1) for k in range(2)]
@@ -185,23 +213,29 @@
         return done
 
     bands = w.shape[2]
+    outer_base = odd * (2 * HALO + blocks)
+    inner_base = (1 - odd) * (2 * HALO + blocks)
     shift_a = [offs[0, b] + HALO for b in range(bands)]
     shift_b = [offs[1, b] + HALO for b in range(bands)]
 
     @pl.loop(0, chunks)
     def _(c):
-        @pl.when(c + AHEAD < chunks)
-        def _():
-            receive(c + AHEAD)
+        @pl.when(c + INNER < chunks)
+        def _():
+            receive_inner(c + INNER)
+
+        @pl.when(c + OUTER < chunks)
+        def _():
+            receive_outer(c + OUTER)
 
         for j in range(blocks):
             work[2 * HALO + j] = zin[c, :, j * size : (j + 1) * size]
-        to_left(c).wait_recv()
+        to_inner(c).wait_recv()
         for j in range(2 * HALO):
-            work[2 * HALO + blocks + j] = hr[c, :, j * size : (j + 1) * size]
-        to_right(c).wait_recv()
+            work[inner_base + j] = hi[c, :, j * size : (j + 1) * size]
+        to_outer(c).wait_recv()
         for j in range(2 * HALO):
-            work[j] = hl[c, :, j * size : (j + 1) * size]
+            work[outer_base + j] = ho[c, :, j * size : (j + 1) * size]
         half = blocks // 2
         for j in range(0, span, 2):
             for k, block in enumerate(apply(work, wa, j, j, shift_a, j)):
@@ -216,6 +250,7 @@
 
         @pl.when(jnp.logical_not(last))
         def _():
+            forward_edge(c).start()
             forward(c).start()
 
         @pl.when(last)
@@ -230,11 +265,12 @@
 
     @pl.loop(0, chunks)
     def _(c):
-        to_left(c).wait_send()
-        to_right(c).wait_send()
+        to_outer(c).wait_send()
+        to_inner(c).wait_send()
 
         @pl.when(jnp.logical_not(last))
         def _():
+            forward_edge(c).wait_send()
             forward(c).wait_send()
 
         @pl.when(last)
@@ -285,7 +321,7 @@
             pltpu.VMEM((span + 2 * HALO, ROWS, size), bf16),
             pltpu.VMEM((blocks // 2 + 2 * HALO, ROWS, size), bf16),
             pltpu.VMEM((blocks // 2 + 2 * HALO, ROWS, size), bf16),
-            dma((chunks,)), dma((chunks,)), dma((chunks,)), dma((chunks,)), dma((chunks,)), dma((chunks,)),
+            *[dma((chunks,))] * 8,
             dma((micro * share // ROWS,)), dma((6,)), dma((4,)),
         ],
         compiler_params=pltpu.CompilerParams(collective_id=0, has_side_effects=True),

time: 116 us -> 113 us (0.974)
  Pallas kernels: 114 us -> 111 us
    pallas_call x1, Pallas kernels: 114 us -> 111 us  [shards(): pl.pallas_call(functools.partial(kernel, dims), out_shape=jax.ShapeDtypeS...]
where the time goes in v3:
time: 113 us; the launch traced here: 112 us
  Pallas kernels  111 us (98%)
  local copies, waits for them, and re-layouts  1.67 us (1%)
    pallas_call x1, Pallas kernels, shards(): pl.pallas_call(functools.partial(kernel, dims), out_shape=jax.ShapeDtypeS...  111 us

profile of v3, /device:TPU:224, one launch (start us, length us, event | category | flops | bytes accessed | tf_op | source)
XLA Modules:
  0.0 112.4 jit_solution(3581906253471067898)
XLA Ops:
  0.0 110.7 %shard_map.46 = bf16[2,32,2048]{2,1,0:T(8,128)(2,1)} custom-call(s32[2,3]{1,0:T(2,128)} %offs.1, bf16[2,256,2048]{2,1,0:T(8,128)(2,1)} %x.1, bf16[2,16,3,128,128]{4,3,2,1,0:T(8,128)(2,1)} %w.1, bf16[2,2048]{1,0:T(2,128)(2,1)} %bias.1), custom_call_target="tpu_custom_call" | custom-call | tf_op jit(solution)/shard_map/pallas_call | solution.py:301
  110.7 1.7 %copy.6 = bf16[2,32,2048]{2,1,0:T(8,128)(2,1)} copy(bf16[2,32,2048]{2,1,0:T(8,128)(2,1)} %shard_map.46) | data formatting | bytes 524288

commit v4 on v3

--- a/solution.py
+++ b/solution.py
@@ -12,12 +12,14 @@
 ceiling = 2.0
 ROWS = 16
 OUTER = 3
-INNER = 2
+FIRST = 3
+INNER = FIRST + 1
+SLOTS = FIRST + 1
 
 
 def kernel(
     dims, offs, x, w, bias, out,
-    wa, wb, bl, br, bs, zin, zout, ho, hi, work, mid_low, mid_high,
+    wa, wb, bo, bi, bs, zin, zout, ho, hi, work, mid,
     es, er, zs, zr, os, orr, ks, kr, og, ws, wr,
 ):
     sections, devices, micro, share, chunks, blocks, size = dims
@@ -102,7 +104,7 @@
 
     @pl.when(first)
     def _():
-        for c in range(OUTER):
+        for c in range(INNER):
             fetch(c).start()
 
     own_a = pltpu.make_async_copy(w.at[0], wa.at[pl.ds(HALO, blocks)], ws.at[0])
@@ -112,7 +114,7 @@
 
     @pl.when(first)
     def _():
-        @pl.loop(OUTER, chunks)
+        @pl.loop(INNER, chunks)
         def _(c):
             fetch(c).start()
 
@@ -126,91 +128,134 @@
 
 
     def receive_outer(c):
+        @pl.when(jnp.logical_not(first))
+        def _():
+            forward_edge(c).wait_recv()
+
+        to_outer(c).start()
+
+    def receive_inner(c):
         @pl.when(first)
         def _():
             fetch(c).wait()
 
         @pl.when(jnp.logical_not(first))
         def _():
-            forward_edge(c).wait_recv()
-
-        to_outer(c).start()
-
-    def receive_inner(c):
-        @pl.when(jnp.logical_not(first))
-        def _():
             forward(c).wait_recv()
 
         to_inner(c).start()
 
-    def receive_first():
-        for c in range(OUTER):
-            receive_outer(c)
-            if c < INNER:
-                receive_inner(c)
-
-    edge_left = pltpu.make_async_remote_copy(
-        src_ref=w.at[0, pl.ds(0, HALO)], dst_ref=wa.at[pl.ds(HALO + blocks, HALO)],
-        send_sem=ws.at[2], recv_sem=wr.at[0], device_id={"neuron": left}, device_id_type=MESH)
-    edge_right = pltpu.make_async_remote_copy(
-        src_ref=w.at[0, pl.ds(blocks - HALO, HALO)], dst_ref=wa.at[pl.ds(0, HALO)],
-        send_sem=ws.at[3], recv_sem=wr.at[1], device_id={"neuron": right}, device_id_type=MESH)
-    bias_left = pltpu.make_async_remote_copy(
-        src_ref=bias.at[:, pl.ds(0, HALO * size)], dst_ref=br,
-        send_sem=ws.at[4], recv_sem=wr.at[2], device_id={"neuron": left}, device_id_type=MESH)
-    bias_right = pltpu.make_async_remote_copy(
-        src_ref=bias.at[:, pl.ds((blocks - HALO) * size, HALO * size)], dst_ref=bl,
-        send_sem=ws.at[5], recv_sem=wr.at[3], device_id={"neuron": right}, device_id_type=MESH)
-    edges = (bias_left, bias_right, edge_left, edge_right)
-    for copy in edges:
+    def margin(k, source, target, device):
+        return pltpu.make_async_remote_copy(
+            src_ref=source, dst_ref=target, send_sem=ws.at[2 + k], recv_sem=wr.at[k],
+            device_id={"neuron": device}, device_id_type=MESH)
+
+    own_end = blocks - HALO
+    outer_block, inner_block = odd * own_end, (1 - odd) * own_end
+    edge_width = HALO * size
+
+    def columns(block):
+        return pl.ds(pl.multiple_of(block * size, size), edge_width)
+
+    outer_margin = (1 - odd) * (HALO + blocks)
+    inner_margin = odd * (HALO + blocks)
+    inner_bias = margin(0, bias.at[:, columns(inner_block)], bi, inner)
+    inner_weights = margin(1, w.at[0, pl.ds(inner_block, HALO)], wa.at[pl.ds(inner_margin, HALO)], inner)
+    outer_bias = margin(2, bias.at[:, columns(outer_block)], bo, outer)
+    outer_weights = margin(3, w.at[0, pl.ds(outer_block, HALO)], wa.at[pl.ds(outer_margin, HALO)], outer)
+
+    @pl.when(first)
+    def _():
+        receive_inner(0)
+        receive_outer(0)
+
+    for copy in (inner_bias, inner_weights, outer_bias, outer_weights):
         copy.start()
 
     @pl.when(first)
     def _():
-        receive_first()
-
-    for copy in (bias_left, bias_right):
-        copy.wait()
+        for c in range(1, INNER):
+            receive_inner(c)
+            if c < OUTER:
+                receive_outer(c)
+
     span = blocks + 2 * HALO
+
+    def bias_rows(values, row, start, block):
+        bs[start] = jnp.broadcast_to(values[row : row + 1, block * size : (block + 1) * size], (rows, size))
+
     own = bias[...].astype(jnp.float32)
-    from_left = bl[...].astype(jnp.float32)
-    from_right = br[...].astype(jnp.float32)
+    for j in range(blocks):
+        bias_rows(own, 0, HALO + j, j)
+        bias_rows(own, 1, span + j, j)
+    inner_bias.wait()
+    arrived = bi[...].astype(jnp.float32)
     for j in range(HALO):
-        bs[j : j + 1, :] = from_left[0:1, j * size : (j + 1) * size]
-        bs[HALO + blocks + j : HALO + blocks + j + 1, :] = from_right[0:1, j * size : (j + 1) * size]
-    for j in range(blocks):
-        bs[HALO + j : HALO + j + 1, :] = own[0:1, j * size : (j + 1) * size]
-        bs[span + j : span + j + 1, :] = own[1:2, j * size : (j + 1) * size]
+        bias_rows(arrived, 0, (1 - odd) * (HALO + blocks) + j, j)
     own_a.wait()
     own_b.wait()
-    edge_left.wait()
-    edge_right.wait()
-
-    @pl.when(jnp.logical_not(first))
-    def _():
-        receive_first()
-
-    def apply(source, weights, j, at, shift, bias_row):
-        low = [jnp.concatenate([source[at + k + s] for s in shift[:2]], axis=1) for k in range(2)]
+    inner_weights.wait()
+
+    def apply(source, at, weights, pair, shift, bias_base):
         sums = [
-            jnp.dot(low[k], weights[j + k, 0:2].reshape(2 * size, size), preferred_element_type=jnp.float32)
-            for k in range(2)
+            jnp.dot(
+                jnp.concatenate([source[at + p + s] for s in shift[:2]], axis=1),
+                weights[p, 0:2].reshape(2 * size, size),
+                preferred_element_type=jnp.float32,
+            )
+            for p in pair
         ]
         zero = jnp.zeros((rows, size), jnp.bfloat16)
         third = jnp.concatenate(
             [
-                jnp.concatenate([source[at + shift[2]], zero], axis=1),
-                jnp.concatenate([zero, source[at + 1 + shift[2]]], axis=1),
+                jnp.concatenate([source[at + pair[0] + shift[2]], zero], axis=1),
+                jnp.concatenate([zero, source[at + pair[1] + shift[2]]], axis=1),
             ],
             axis=0,
         )
-        both = jnp.concatenate([weights[j, 2], weights[j + 1, 2]], axis=0)
+        both = jnp.concatenate([weights[p, 2] for p in pair], axis=0)
         rest = jnp.dot(third, both, preferred_element_type=jnp.float32)
         done = []
-        for k in range(2):
-            total = sums[k] + rest[k * rows : (k + 1) * rows] + bs[bias_row + k : bias_row + k + 1, :]
+        for k, p in enumerate(pair):
+            total = sums[k] + rest[k * rows : (k + 1) * rows] + bs[bias_base + p]
             done.append(jnp.minimum(jnp.maximum(total, 0.0), ceiling).astype(jnp.bfloat16))
         return done
+
+    reach = span + 2 * HALO
+
+    def layer_a(slot, begin, end):
+        for j in range(begin, end, 2):
+            pair = [k + odd * (span - 1 - 2 * k) for k in (j, j + 1)]
+            for p, block in zip(pair, apply(work, slot * reach, wa, pair, shift_a, 0)):
+                mid[slot * span + p] = block
+
+    def layer_b(c, slot, begin, end):
+        for j in range(begin, end, 2):
+            pair = [k + odd * (blocks - 1 - 2 * k) for k in (j, j + 1)]
+            for p, block in zip(pair, apply(mid, slot * span, wb, pair, shift_b, span)):
+                zout[c, :, pl.ds(pl.multiple_of(p * size, size), size)] = block
+
+    def first_phase(c):
+        slot = c % SLOTS
+        for j in range(blocks):
+            work[slot * reach + 2 * HALO + j] = zin[c, :, j * size : (j + 1) * size]
+        to_inner(c).wait_recv()
+        for j in range(2 * HALO):
+            work[slot * reach + inner_base + j] = hi[c, :, j * size : (j + 1) * size]
+        layer_a(slot, 2 * HALO, span)
+        layer_b(c, slot, 2 * HALO, blocks)
+
+        @pl.when(jnp.logical_not(last))
+        def _():
+            forward(c).start()
+
+    def second_phase(c):
+        slot = c % SLOTS
+        to_outer(c).wait_recv()
+        for j in range(2 * HALO):
+            work[slot * reach + outer_base + j] = ho[c, :, j * size : (j + 1) * size]
+        layer_a(slot, 0, 2 * HALO)
+        layer_b(c, slot, 0, 2 * HALO)
 
     bands = w.shape[2]
     outer_base = odd * (2 * HALO + blocks)
@@ -218,40 +263,52 @@
     shift_a = [offs[0, b] + HALO for b in range(bands)]
     shift_b = [offs[1, b] + HALO for b in range(bands)]
 
+    later = jnp.logical_not(first)
+
+    @pl.when(later)
+    def _():
+        for c in range(FIRST):
+            receive_inner(c)
+        receive_outer(0)
+
+    first_phase(0)
+    for c in range(1, FIRST):
+        @pl.when(later)
+        def _(c=c):
+            if c == 1:
+                receive_inner(FIRST)
+            if c < OUTER:
+                receive_outer(c)
+
+        first_phase(c)
+
+    @pl.when(later)
+    def _():
+        for c in range(max(FIRST, 1), OUTER):
+            receive_outer(c)
+        if FIRST == 1:
+            receive_inner(FIRST)
+
+    outer_bias.wait()
+    arrived = bo[...].astype(jnp.float32)
+    for j in range(HALO):
+        bias_rows(arrived, 0, odd * (HALO + blocks) + j, j)
+    outer_weights.wait()
+
+    far = jnp.logical_or(me == 0, me == devices - 1)
+    close = jnp.logical_not(far)
+
     @pl.loop(0, chunks)
     def _(c):
-        @pl.when(c + INNER < chunks)
-        def _():
-            receive_inner(c + INNER)
-
-        @pl.when(c + OUTER < chunks)
+        @pl.when(jnp.logical_and(far, c + OUTER < chunks))
         def _():
             receive_outer(c + OUTER)
 
-        for j in range(blocks):
-            work[2 * HALO + j] = zin[c, :, j * size : (j + 1) * size]
-        to_inner(c).wait_recv()
-        for j in range(2 * HALO):
-            work[inner_base + j] = hi[c, :, j * size : (j + 1) * size]
-        to_outer(c).wait_recv()
-        for j in range(2 * HALO):
-            work[outer_base + j] = ho[c, :, j * size : (j + 1) * size]
-        half = blocks // 2
-        for j in range(0, span, 2):
-            for k, block in enumerate(apply(work, wa, j, j, shift_a, j)):
-                if j + k < half + 2 * HALO:
-                    mid_low[j + k] = block
-                if j + k >= half:
-                    mid_high[j + k - half] = block
-        for j in range(0, blocks, 2):
-            source, at = (mid_low, j) if j < half else (mid_high, j - half)
-            for k, block in enumerate(apply(source, wb, j, at, shift_b, span + j)):
-                zout[c, :, (j + k) * size : (j + k + 1) * size] = block
+        second_phase(c)
 
         @pl.when(jnp.logical_not(last))
         def _():
             forward_edge(c).start()
-            forward(c).start()
 
         @pl.when(last)
         def _():
@@ -262,6 +319,18 @@
             @pl.when(c // per_owner == sections - 1)
             def _():
                 keep(c).start()
+
+        @pl.when(c + INNER < chunks)
+        def _():
+            receive_inner(c + INNER)
+
+        @pl.when(jnp.logical_and(close, c + OUTER < chunks))
+        def _():
+            receive_outer(c + OUTER)
+
+        @pl.when(c + FIRST < chunks)
+        def _():
+            first_phase(c + FIRST)
 
     @pl.loop(0, chunks)
     def _(c):
@@ -313,14 +382,13 @@
             pltpu.VMEM((blocks, bands, size, size), bf16),
             pltpu.VMEM((layers, HALO * size), bf16),
             pltpu.VMEM((layers, HALO * size), bf16),
-            pltpu.VMEM((span + blocks + 2, size), jnp.float32),
+            pltpu.VMEM((span + blocks, ROWS, size), jnp.float32),
             pltpu.VMEM((chunks, ROWS, local), bf16),
             pltpu.VMEM((chunks, ROWS, local), bf16),
             pltpu.VMEM((chunks, ROWS, 2 * HALO * size), bf16),
             pltpu.VMEM((chunks, ROWS, 2 * HALO * size), bf16),
-            pltpu.VMEM((span + 2 * HALO, ROWS, size), bf16),
-            pltpu.VMEM((blocks // 2 + 2 * HALO, ROWS, size), bf16),
-            pltpu.VMEM((blocks // 2 + 2 * HALO, ROWS, size), bf16),
+            pltpu.VMEM((SLOTS * (span + 2 * HALO), ROWS, size), bf16),
+            pltpu.VMEM((SLOTS * span, ROWS, size), bf16),
             *[dma((chunks,))] * 8,
             dma((micro * share // ROWS,)), dma((6,)), dma((4,)),
         ],

time: 113 us -> 111 us (0.982)
  Pallas kernels: 111 us -> 109 us
    pallas_call x1, Pallas kernels: 111 us -> 109 us  [shards(): pl.pallas_call(functools.partial(kernel, dims), out_shape=jax.ShapeDtypeS...]
where the time goes in v4:
time: 111 us; the launch traced here: 110 us
  Pallas kernels  109 us (98%)
  local copies, waits for them, and re-layouts  1.67 us (2%)
    pallas_call x1, Pallas kernels, shards(): pl.pallas_call(functools.partial(kernel, dims), out_shape=jax.ShapeDtypeS...  109 us

profile of v4, /device:TPU:224, one launch (start us, length us, event | category | flops | bytes accessed | tf_op | source)
XLA Modules:
  0.0 110.4 jit_solution(13846947600420811668)
XLA Ops:
  0.0 108.8 %shard_map.46 = bf16[2,32,2048]{2,1,0:T(8,128)(2,1)} custom-call(s32[2,3]{1,0:T(2,128)} %offs.1, bf16[2,256,2048]{2,1,0:T(8,128)(2,1)} %x.1, bf16[2,16,3,128,128]{4,3,2,1,0:T(8,128)(2,1)} %w.1, bf16[2,2048]{1,0:T(2,128)(2,1)} %bias.1), custom_call_target="tpu_custom_call" | custom-call | tf_op jit(solution)/shard_map/pallas_call | solution.py:370
  108.8 1.7 %copy.6 = bf16[2,32,2048]{2,1,0:T(8,128)(2,1)} copy(bf16[2,32,2048]{2,1,0:T(8,128)(2,1)} %shard_map.46) | data formatting | bytes 524288

commit v5 on v4

--- a/solution.py
+++ b/solution.py
@@ -12,6 +12,7 @@
 ceiling = 2.0
 ROWS = 16
 OUTER = 3
+REUSE = 8
 FIRST = 3
 INNER = FIRST + 1
 SLOTS = FIRST + 1
@@ -71,35 +72,35 @@
     def forward_edge(c):
         cut = pl.ds(outer_start, width)
         return pltpu.make_async_remote_copy(
-            src_ref=zout.at[c, :, cut], dst_ref=zin.at[c, :, cut], send_sem=es.at[c], recv_sem=er.at[c],
+            src_ref=zout.at[c, :, cut], dst_ref=zin.at[c, :, cut], send_sem=es.at[c % REUSE], recv_sem=er.at[c],
             device_id={"section": after}, device_id_type=MESH)
 
     def forward(c):
         cut = pl.ds(rest_start, rest)
         return pltpu.make_async_remote_copy(
-            src_ref=zout.at[c, :, cut], dst_ref=zin.at[c, :, cut], send_sem=zs.at[c], recv_sem=zr.at[c],
+            src_ref=zout.at[c, :, cut], dst_ref=zin.at[c, :, cut], send_sem=zs.at[c % REUSE], recv_sem=zr.at[c],
             device_id={"section": after}, device_id_type=MESH)
 
     def deliver(c):
         owner, slot, batch, row = place(c)
         target = out.at[batch, pl.ds(pl.multiple_of(row, rows), rows), :]
         return pltpu.make_async_remote_copy(
-            src_ref=zout.at[c], dst_ref=target, send_sem=zs.at[c], recv_sem=og.at[slot],
+            src_ref=zout.at[c], dst_ref=target, send_sem=zs.at[c % REUSE], recv_sem=og.at[slot],
             device_id={"section": owner}, device_id_type=MESH)
 
     def keep(c):
         _, _, batch, row = place(c)
         target = out.at[batch, pl.ds(pl.multiple_of(row, rows), rows), :]
-        return pltpu.make_async_copy(zout.at[c], target, zs.at[c])
+        return pltpu.make_async_copy(zout.at[c], target, zs.at[c % REUSE])
 
     def to_outer(c):
         return pltpu.make_async_remote_copy(
-            src_ref=zin.at[c, :, pl.ds(outer_start, width)], dst_ref=ho.at[c], send_sem=os.at[c], recv_sem=orr.at[c],
+            src_ref=zin.at[c, :, pl.ds(outer_start, width)], dst_ref=ho.at[c], send_sem=os.at[c % REUSE], recv_sem=orr.at[c],
             device_id={"neuron": outer}, device_id_type=MESH)
 
     def to_inner(c):
         return pltpu.make_async_remote_copy(
-            src_ref=zin.at[c, :, pl.ds(inner_start, width)], dst_ref=hi.at[c], send_sem=ks.at[c], recv_sem=kr.at[c],
+            src_ref=zin.at[c, :, pl.ds(inner_start, width)], dst_ref=hi.at[c], send_sem=ks.at[c % REUSE], recv_sem=kr.at[c],
             device_id={"neuron": inner}, device_id_type=MESH)
 
     @pl.when(first)
@@ -132,6 +133,11 @@
         def _():
             forward_edge(c).wait_recv()
 
+        if not isinstance(c, int):
+            @pl.when(c >= REUSE)
+            def _():
+                to_outer(c - REUSE).wait_send()
+
         to_outer(c).start()
 
     def receive_inner(c):
@@ -142,6 +148,11 @@
         @pl.when(jnp.logical_not(first))
         def _():
             forward(c).wait_recv()
+
+        if not isinstance(c, int):
+            @pl.when(c >= REUSE)
+            def _():
+                to_inner(c - REUSE).wait_send()
 
         to_inner(c).start()
 
@@ -247,6 +258,11 @@
 
         @pl.when(jnp.logical_not(last))
         def _():
+            if not isinstance(c, int):
+                @pl.when(c >= REUSE)
+                def _():
+                    forward(c - REUSE).wait_send()
+
             forward(c).start()
 
     def second_phase(c):
@@ -308,16 +324,25 @@
 
         @pl.when(jnp.logical_not(last))
         def _():
+            @pl.when(c >= REUSE)
+            def _():
+                forward_edge(c - REUSE).wait_send()
+
             forward_edge(c).start()
 
         @pl.when(last)
         def _():
             @pl.when(c // per_owner < sections - 1)
             def _():
+                @pl.when(c >= REUSE)
+                def _():
+                    deliver(c - REUSE).wait_send()
+
                 deliver(c).start()
 
             @pl.when(c // per_owner == sections - 1)
             def _():
+                deliver(c - REUSE).wait_send()
                 keep(c).start()
 
         @pl.when(c + INNER < chunks)
@@ -332,7 +357,7 @@
         def _():
             first_phase(c + FIRST)
 
-    @pl.loop(0, chunks)
+    @pl.loop(chunks - REUSE, chunks)
     def _(c):
         to_outer(c).wait_send()
         to_inner(c).wait_send()
@@ -389,7 +414,7 @@
             pltpu.VMEM((chunks, ROWS, 2 * HALO * size), bf16),
             pltpu.VMEM((SLOTS * (span + 2 * HALO), ROWS, size), bf16),
             pltpu.VMEM((SLOTS * span, ROWS, size), bf16),
-            *[dma((chunks,))] * 8,
+            *[dma((REUSE,)), dma((chunks,))] * 2, *[dma((REUSE,)), dma((chunks,))] * 2,
             dma((micro * share // ROWS,)), dma((6,)), dma((4,)),
         ],
         compiler_params=pltpu.CompilerParams(collective_id=0, has_side_effects=True),

time: 111 us -> 110 us (level)
  no operation moved by 1% of the time
where the time goes in v5:
time: 110 us
  Pallas kernels  108 us (98%)
  local copies, waits for them, and re-layouts  1.67 us (2%)
    pallas_call x1, Pallas kernels, shards(): pl.pallas_call(functools.partial(kernel, dims), out_shape=jax.ShapeDtypeS...  108 us

profile of v5, /device:TPU:224, one launch (start us, length us, event | category | flops | bytes accessed | tf_op | source)
XLA Modules:
  0.0 109.5 jit_solution(9654326099595768472)
XLA Ops:
  0.0 107.8 %shard_map.46 = bf16[2,32,2048]{2,1,0:T(8,128)(2,1)} custom-call(s32[2,3]{1,0:T(2,128)} %offs.1, bf16[2,256,2048]{2,1,0:T(8,128)(2,1)} %x.1, bf16[2,16,3,128,128]{4,3,2,1,0:T(8,128)(2,1)} %w.1, bf16[2,2048]{1,0:T(2,128)(2,1)} %bias.1), custom_call_target="tpu_custom_call" | custom-call | tf_op jit(solution)/shard_map/pallas_call | solution.py:395
  107.8 1.7 %copy.6 = bf16[2,32,2048]{2,1,0:T(8,128)(2,1)} copy(bf16[2,32,2048]{2,1,0:T(8,128)(2,1)} %shard_map.46) | data formatting | bytes 524288

commit v6 on v5

--- a/solution.py
+++ b/solution.py
@@ -95,12 +95,12 @@
 
     def to_outer(c):
         return pltpu.make_async_remote_copy(
-            src_ref=zin.at[c, :, pl.ds(outer_start, width)], dst_ref=ho.at[c], send_sem=os.at[c % REUSE], recv_sem=orr.at[c],
+            src_ref=zin.at[c, :, pl.ds(outer_start, width)], dst_ref=ho.at[c], send_sem=os.at[c % REUSE], recv_sem=orr.at[c % REUSE],
             device_id={"neuron": outer}, device_id_type=MESH)
 
     def to_inner(c):
         return pltpu.make_async_remote_copy(
-            src_ref=zin.at[c, :, pl.ds(inner_start, width)], dst_ref=hi.at[c], send_sem=ks.at[c % REUSE], recv_sem=kr.at[c],
+            src_ref=zin.at[c, :, pl.ds(inner_start, width)], dst_ref=hi.at[c], send_sem=ks.at[c % REUSE], recv_sem=kr.at[c % REUSE],
             device_id={"neuron": inner}, device_id_type=MESH)
 
     @pl.when(first)
@@ -414,7 +414,7 @@
             pltpu.VMEM((chunks, ROWS, 2 * HALO * size), bf16),
             pltpu.VMEM((SLOTS * (span + 2 * HALO), ROWS, size), bf16),
             pltpu.VMEM((SLOTS * span, ROWS, size), bf16),
-            *[dma((REUSE,)), dma((chunks,))] * 2, *[dma((REUSE,)), dma((chunks,))] * 2,
+            *[dma((REUSE,)), dma((chunks,))] * 2, *[dma((REUSE,))] * 4,
             dma((micro * share // ROWS,)), dma((6,)), dma((4,)),
         ],
         compiler_params=pltpu.CompilerParams(collective_id=0, has_side_effects=True),

time: 110 us -> 109 us (level)
  no operation moved by 1% of the time
where the time goes in v6:
time: 109 us
  Pallas kernels  107 us (98%)
  local copies, waits for them, and re-layouts  1.67 us (2%)
    pallas_call x1, Pallas kernels, shards(): pl.pallas_call(functools.partial(kernel, dims), out_shape=jax.ShapeDtypeS...  107 us

profile of v6, /device:TPU:224, one launch (start us, length us, event | category | flops | bytes accessed | tf_op | source)
XLA Modules:
  0.0 109.1 jit_solution(12722541260102819719)
XLA Ops:
  0.0 107.4 %shard_map.46 = bf16[2,32,2048]{2,1,0:T(8,128)(2,1)} custom-call(s32[2,3]{1,0:T(2,128)} %offs.1, bf16[2,256,2048]{2,1,0:T(8,128)(2,1)} %x.1, bf16[2,16,3,128,128]{4,3,2,1,0:T(8,128)(2,1)} %w.1, bf16[2,2048]{1,0:T(2,128)(2,1)} %bias.1), custom_call_target="tpu_custom_call" | custom-call | tf_op jit(solution)/shard_map/pallas_call | solution.py:395
  107.4 1.7 %copy.6 = bf16[2,32,2048]{2,1,0:T(8,128)(2,1)} copy(bf16[2,32,2048]{2,1,0:T(8,128)(2,1)} %shard_map.46) | data formatting | bytes 524288
